TPU v7x, 32 devices: a whole 2x2x4 slice. The times are simulated.
32 devices in a mesh: dp: 8 (over z, core), seq: 4 (over y, x).
Axes of the slice: x: 2, y: 2, z: 4, core: 2. Of those that a mesh axis runs over, the one named last changes fastest.
Arguments:
- inputs: bfloat16 [24, 512, 1024], P('dp', 'seq'), may hold values from -6 to 6
- w_query: bfloat16 [1024, 1024], P('dp'), may hold values from -0.1875 to 0.1875
- w_key: bfloat16 [1024, 1024], P('dp'), may hold values from -0.1875 to 0.1875
- w_value: bfloat16 [1024, 1024], P('dp'), may hold values from -0.1875 to 0.1875
- b_query: bfloat16 [1024], P('dp'), may hold values from -4 to 4
- b_value: bfloat16 [1024], P('dp'), may hold values from -0.75 to 0.75
- w_out: bfloat16 [1024, 1024], P('dp'), may hold values from -2.5 to 2.5
- b_out: bfloat16 [1024], P('dp'), may hold values from -4 to 4
- gain_one: bfloat16 [1024], P('dp'), may hold values from 0.5 to 1.5
- shift_one: bfloat16 [1024], P('dp'), may hold values from -4 to 4
- w_up: bfloat16 [1024, 4096], P('dp'), may hold values from -0.1875 to 0.1875
- b_up: bfloat16 [4096], P('dp'), may hold values from -6 to 6
- w_down: bfloat16 [4096, 1024], P('dp'), may hold values from -0.09375 to 0.09375
- b_down: bfloat16 [1024], P('dp'), may hold values from -4 to 4
- gain_two: bfloat16 [1024], P('dp'), may hold values from 0.5 to 1.5
- shift_two: bfloat16 [1024], P('dp'), may hold values from -4 to 4
- cotangent: bfloat16 [24, 512, 1024], P('dp', 'seq'), may hold values from -6 to 6
Outputs:
- output: bfloat16 [24, 512, 1024], P('dp', 'seq')
- grad_inputs: float32 [24, 512, 1024], P('dp', 'seq')
- grad_w_query: float32 [1024, 1024], P('dp')
- grad_w_key: float32 [1024, 1024], P('dp')
- grad_w_value: float32 [1024, 1024], P('dp')
- grad_b_query: float32 [1024], P('dp')
- grad_b_value: float32 [1024], P('dp')
- grad_w_out: float32 [1024, 1024], P('dp')
- grad_b_out: float32 [1024], P('dp')
- grad_gain_one: float32 [1024], P('dp')
- grad_shift_one: float32 [1024], P('dp')
- grad_w_up: float32 [1024, 4096], P('dp')
- grad_b_up: float32 [4096], P('dp')
- grad_w_down: float32 [4096, 1024], P('dp')
- grad_b_down: float32 [1024], P('dp')
- grad_gain_two: float32 [1024], P('dp')
- grad_shift_two: float32 [1024], P('dp')
All inputs are finite; a program needn't handle non-finite values.
Results may differ from a plain program's by a relative error of at most 0.02.
Values may be sent and summed in bfloat16 or wider, within the bound.
No kernel may reach another device: no remote copies, remote signals or barrier semaphores. Data moves between devices by JAX's collectives and lax.ppermute only.
A program may use at most 192 MiB of HBM per device.

v0:
```python
import jax
import jax.numpy as jnp
from jax import lax
from jax.sharding import PartitionSpec as P

HEAD_DIM = 64
EPSILON = 1e-12


def dot_rows(former, latter):
    return jnp.dot(former, latter, preferred_element_type=jnp.float32)


def dot_left(former, latter):
    return lax.dot_general(
        former, latter, (((0,), (0,)), ((), ())), preferred_element_type=jnp.float32
    )


def dot_right(former, latter):
    return lax.dot_general(
        former, latter, (((1,), (1,)), ((), ())), preferred_element_type=jnp.float32
    )


def normalize(hidden, gain_vec, offset):
    center = hidden - jnp.mean(hidden, -1, keepdims=True)
    spread = jnp.mean(center * center, -1, keepdims=True)
    return center * lax.rsqrt(spread + EPSILON) * gain_vec + offset


def normalize_back(hidden, gain_vec, offset, upstream):
    result, pullback = jax.vjp(normalize, hidden, gain_vec, offset)
    return pullback(upstream)


def activation(hidden):
    return jax.nn.gelu(hidden, approximate=False)


def activation_back(hidden, upstream):
    result, pullback = jax.vjp(activation, hidden)
    return pullback(upstream)[0]


def attend(head_query, head_key, head_value):
    groups, length, columns = head_query.shape
    four_dims = (groups, length, columns // HEAD_DIM, HEAD_DIM)
    factor = HEAD_DIM ** (-0.5)
    scores = (
        jnp.einsum(
            "gqhd,gkhd->ghqk",
            head_query.reshape(four_dims),
            head_key.reshape(four_dims),
            preferred_element_type=jnp.float32,
        )
        * factor
    )
    row_max = jnp.max(scores, -1, keepdims=True)
    exponent = jnp.exp(scores - row_max)
    row_total = jnp.sum(exponent, -1, keepdims=True)
    portions_low = (exponent / row_total).astype(jnp.bfloat16)
    context = jnp.einsum(
        "ghqk,gkhd->gqhd",
        portions_low,
        head_value.reshape(four_dims),
        preferred_element_type=jnp.float32,
    )
    return (
        context.astype(jnp.bfloat16).reshape(groups, length, columns),
        row_max + jnp.log(row_total),
    )


def attend_back(head_query, head_key, head_value, log_total, upstream):
    groups, length, columns = head_query.shape
    four_dims = (groups, length, columns // HEAD_DIM, HEAD_DIM)
    factor = HEAD_DIM ** (-0.5)
    query_four = head_query.reshape(four_dims)
    key_four = head_key.reshape(four_dims)
    upstream_four = upstream.reshape(four_dims)
    scores = (
        jnp.einsum("gqhd,gkhd->ghqk", query_four, key_four, preferred_element_type=jnp.float32)
        * factor
    )
    portions = jnp.exp(scores - log_total)
    portions_low = portions.astype(jnp.bfloat16)
    grad_value = jnp.einsum(
        "ghqk,gqhd->gkhd", portions_low, upstream_four, preferred_element_type=jnp.float32
    )
    grad_portions = jnp.einsum(
        "gqhd,gkhd->ghqk",
        upstream_four,
        head_value.reshape(four_dims),
        preferred_element_type=jnp.float32,
    )
    grad_scores = (
        portions * (grad_portions - jnp.sum(portions * grad_portions, -1, keepdims=True))
    ).astype(jnp.bfloat16)
    grad_query = (
        jnp.einsum("ghqk,gkhd->gqhd", grad_scores, key_four, preferred_element_type=jnp.float32)
        * factor
    )
    grad_key = (
        jnp.einsum("ghqk,gqhd->gkhd", grad_scores, query_four, preferred_element_type=jnp.float32)
        * factor
    )
    three_dims = (groups, length, columns)
    return (
        grad_query.astype(jnp.bfloat16).reshape(three_dims),
        grad_key.astype(jnp.bfloat16).reshape(three_dims),
        grad_value.astype(jnp.bfloat16).reshape(three_dims),
    )


def forward(weights, inputs):
    (
        w_query,
        w_key,
        w_value,
        b_query,
        b_value,
        w_out,
        b_out,
        gain_one,
        shift_one,
        w_up,
        b_up,
        w_down,
        b_down,
        gain_two,
        shift_two,
    ) = weights
    groups, local_len, model_width = inputs.shape
    flat_rows = inputs.reshape(groups * local_len, model_width)
    three_dims = (groups, local_len, model_width)
    queries = (
        (dot_rows(flat_rows, w_query) + b_query.astype(jnp.float32))
        .astype(jnp.bfloat16)
        .reshape(three_dims)
    )
    key_rows = dot_rows(flat_rows, w_key).astype(jnp.bfloat16).reshape(three_dims)
    values = (
        (dot_rows(flat_rows, w_value) + b_value.astype(jnp.float32))
        .astype(jnp.bfloat16)
        .reshape(three_dims)
    )
    head_query, head_key, head_value = (
        lax.all_to_all(queries, "seq", split_axis=2, concat_axis=1, tiled=True),
        lax.all_to_all(key_rows, "seq", split_axis=2, concat_axis=1, tiled=True),
        lax.all_to_all(values, "seq", split_axis=2, concat_axis=1, tiled=True),
    )
    head_context, log_total = attend(head_query, head_key, head_value)
    context = lax.all_to_all(head_context, "seq", split_axis=1, concat_axis=2, tiled=True).reshape(
        groups * local_len, model_width
    )
    first_sum = flat_rows.astype(jnp.float32) + (
        dot_rows(context, w_out) + b_out.astype(jnp.float32)
    )
    normed = normalize(first_sum, gain_one.astype(jnp.float32), shift_one.astype(jnp.float32))
    normed_low = normed.astype(jnp.bfloat16)
    pre_active = dot_rows(normed_low, w_up) + b_up.astype(jnp.float32)
    active = activation(pre_active).astype(jnp.bfloat16)
    second_sum = normed + (dot_rows(active, w_down) + b_down.astype(jnp.float32))
    result = normalize(second_sum, gain_two.astype(jnp.float32), shift_two.astype(jnp.float32))
    stored = (
        flat_rows,
        head_query,
        head_key,
        head_value,
        log_total,
        context,
        first_sum,
        normed_low,
        pre_active,
        active,
        second_sum,
    )
    return (result, stored)


def local(
    inputs,
    w_query,
    w_key,
    w_value,
    b_query,
    b_value,
    w_out,
    b_out,
    gain_one,
    shift_one,
    w_up,
    b_up,
    w_down,
    b_down,
    gain_two,
    shift_two,
    cotangent,
):
    gathered = (
        lax.all_gather(w_query, "dp", axis=0, tiled=True),
        lax.all_gather(w_key, "dp", axis=0, tiled=True),
        lax.all_gather(w_value, "dp", axis=0, tiled=True),
        lax.all_gather(b_query, "dp", axis=0, tiled=True),
        lax.all_gather(b_value, "dp", axis=0, tiled=True),
        lax.all_gather(w_out, "dp", axis=0, tiled=True),
        lax.all_gather(b_out, "dp", axis=0, tiled=True),
        lax.all_gather(gain_one, "dp", axis=0, tiled=True),
        lax.all_gather(shift_one, "dp", axis=0, tiled=True),
        lax.all_gather(w_up, "dp", axis=0, tiled=True),
        lax.all_gather(b_up, "dp", axis=0, tiled=True),
        lax.all_gather(w_down, "dp", axis=0, tiled=True),
        lax.all_gather(b_down, "dp", axis=0, tiled=True),
        lax.all_gather(gain_two, "dp", axis=0, tiled=True),
        lax.all_gather(shift_two, "dp", axis=0, tiled=True),
    )
    result, stored = forward(gathered, inputs)
    output = result.astype(jnp.bfloat16).reshape(inputs.shape)
    weights = (
        lax.all_gather(w_query, "dp", axis=0, tiled=True),
        lax.all_gather(w_key, "dp", axis=0, tiled=True),
        lax.all_gather(w_value, "dp", axis=0, tiled=True),
        lax.all_gather(b_query, "dp", axis=0, tiled=True),
        lax.all_gather(b_value, "dp", axis=0, tiled=True),
        lax.all_gather(w_out, "dp", axis=0, tiled=True),
        lax.all_gather(b_out, "dp", axis=0, tiled=True),
        lax.all_gather(gain_one, "dp", axis=0, tiled=True),
        lax.all_gather(shift_one, "dp", axis=0, tiled=True),
        lax.all_gather(w_up, "dp", axis=0, tiled=True),
        lax.all_gather(b_up, "dp", axis=0, tiled=True),
        lax.all_gather(w_down, "dp", axis=0, tiled=True),
        lax.all_gather(b_down, "dp", axis=0, tiled=True),
        lax.all_gather(gain_two, "dp", axis=0, tiled=True),
        lax.all_gather(shift_two, "dp", axis=0, tiled=True),
    )
    unused, stored = forward(weights, inputs)
    (
        full_query,
        full_key,
        full_value,
        full_bq,
        full_bv,
        full_out,
        full_bo,
        full_gain_one,
        full_shift_one,
        full_up,
        full_bup,
        full_down,
        full_bdown,
        full_gain_two,
        full_shift_two,
    ) = weights
    (
        flat_rows,
        head_query,
        head_key,
        head_value,
        log_total,
        context,
        first_sum,
        normed_low,
        pre_active,
        active,
        second_sum,
    ) = stored
    groups, local_len, model_width = inputs.shape
    upstream = cotangent.reshape(groups * local_len, model_width).astype(jnp.float32)
    grad_second, grad_gain_two, grad_shift_two = normalize_back(
        second_sum, full_gain_two.astype(jnp.float32), full_shift_two.astype(jnp.float32), upstream
    )
    grad_branch_two = grad_second.astype(jnp.bfloat16)
    grad_b_down = jnp.sum(grad_branch_two.astype(jnp.float32), 0)
    grad_w_down = dot_left(active, grad_branch_two)
    grad_pre = activation_back(pre_active, dot_right(grad_branch_two, full_down)).astype(
        jnp.bfloat16
    )
    grad_b_up = jnp.sum(grad_pre.astype(jnp.float32), 0)
    grad_w_up = dot_left(normed_low, grad_pre)
    grad_normed = grad_second + dot_right(grad_pre, full_up)
    grad_first, grad_gain_one, grad_shift_one = normalize_back(
        first_sum,
        full_gain_one.astype(jnp.float32),
        full_shift_one.astype(jnp.float32),
        grad_normed,
    )
    grad_branch_one = grad_first.astype(jnp.bfloat16)
    grad_b_out = jnp.sum(grad_branch_one.astype(jnp.float32), 0)
    grad_w_out = dot_left(context, grad_branch_one)
    grad_context = (
        dot_right(grad_branch_one, full_out)
        .astype(jnp.bfloat16)
        .reshape(groups, local_len, model_width)
    )
    head_grad = lax.all_to_all(grad_context, "seq", split_axis=2, concat_axis=1, tiled=True)
    grad_hq, grad_hk, grad_hv = attend_back(head_query, head_key, head_value, log_total, head_grad)
    grad_queries, grad_keys, grad_values = (
        lax.all_to_all(grad_hq, "seq", split_axis=1, concat_axis=2, tiled=True),
        lax.all_to_all(grad_hk, "seq", split_axis=1, concat_axis=2, tiled=True),
        lax.all_to_all(grad_hv, "seq", split_axis=1, concat_axis=2, tiled=True),
    )
    flat_dims = (groups * local_len, model_width)
    grad_queries = grad_queries.reshape(flat_dims)
    grad_keys = grad_keys.reshape(flat_dims)
    grad_values = grad_values.reshape(flat_dims)
    grad_w_query = dot_left(flat_rows, grad_queries)
    grad_w_key = dot_left(flat_rows, grad_keys)
    grad_w_value = dot_left(flat_rows, grad_values)
    grad_b_query = jnp.sum(grad_queries.astype(jnp.float32), 0)
    grad_b_value = jnp.sum(grad_values.astype(jnp.float32), 0)
    grad_inputs = (
        grad_first
        + dot_right(grad_queries, full_query)
        + dot_right(grad_keys, full_key)
        + dot_right(grad_values, full_value)
    )
    owned_grads = (
        lax.psum_scatter(
            grad_w_query.astype(jnp.bfloat16), "dp", scatter_dimension=0, tiled=True
        ).astype(jnp.float32),
        lax.psum_scatter(
            grad_w_key.astype(jnp.bfloat16), "dp", scatter_dimension=0, tiled=True
        ).astype(jnp.float32),
        lax.psum_scatter(
            grad_w_value.astype(jnp.bfloat16), "dp", scatter_dimension=0, tiled=True
        ).astype(jnp.float32),
        lax.psum_scatter(
            grad_b_query.astype(jnp.bfloat16), "dp", scatter_dimension=0, tiled=True
        ).astype(jnp.float32),
        lax.psum_scatter(
            grad_b_value.astype(jnp.bfloat16), "dp", scatter_dimension=0, tiled=True
        ).astype(jnp.float32),
        lax.psum_scatter(
            grad_w_out.astype(jnp.bfloat16), "dp", scatter_dimension=0, tiled=True
        ).astype(jnp.float32),
        lax.psum_scatter(
            grad_b_out.astype(jnp.bfloat16), "dp", scatter_dimension=0, tiled=True
        ).astype(jnp.float32),
        lax.psum_scatter(
            grad_gain_one.astype(jnp.bfloat16), "dp", scatter_dimension=0, tiled=True
        ).astype(jnp.float32),
        lax.psum_scatter(
            grad_shift_one.astype(jnp.bfloat16), "dp", scatter_dimension=0, tiled=True
        ).astype(jnp.float32),
        lax.psum_scatter(
            grad_w_up.astype(jnp.bfloat16), "dp", scatter_dimension=0, tiled=True
        ).astype(jnp.float32),
        lax.psum_scatter(
            grad_b_up.astype(jnp.bfloat16), "dp", scatter_dimension=0, tiled=True
        ).astype(jnp.float32),
        lax.psum_scatter(
            grad_w_down.astype(jnp.bfloat16), "dp", scatter_dimension=0, tiled=True
        ).astype(jnp.float32),
        lax.psum_scatter(
            grad_b_down.astype(jnp.bfloat16), "dp", scatter_dimension=0, tiled=True
        ).astype(jnp.float32),
        lax.psum_scatter(
            grad_gain_two.astype(jnp.bfloat16), "dp", scatter_dimension=0, tiled=True
        ).astype(jnp.float32),
        lax.psum_scatter(
            grad_shift_two.astype(jnp.bfloat16), "dp", scatter_dimension=0, tiled=True
        ).astype(jnp.float32),
    )
    summed = (
        lax.psum(owned_grads[0].astype(jnp.bfloat16), "seq").astype(jnp.float32),
        lax.psum(owned_grads[1].astype(jnp.bfloat16), "seq").astype(jnp.float32),
        lax.psum(owned_grads[2].astype(jnp.bfloat16), "seq").astype(jnp.float32),
        lax.psum(owned_grads[3].astype(jnp.bfloat16), "seq").astype(jnp.float32),
        lax.psum(owned_grads[4].astype(jnp.bfloat16), "seq").astype(jnp.float32),
        lax.psum(owned_grads[5].astype(jnp.bfloat16), "seq").astype(jnp.float32),
        lax.psum(owned_grads[6].astype(jnp.bfloat16), "seq").astype(jnp.float32),
        lax.psum(owned_grads[7].astype(jnp.bfloat16), "seq").astype(jnp.float32),
        lax.psum(owned_grads[8].astype(jnp.bfloat16), "seq").astype(jnp.float32),
        lax.psum(owned_grads[9].astype(jnp.bfloat16), "seq").astype(jnp.float32),
        lax.psum(owned_grads[10].astype(jnp.bfloat16), "seq").astype(jnp.float32),
        lax.psum(owned_grads[11].astype(jnp.bfloat16), "seq").astype(jnp.float32),
        lax.psum(owned_grads[12].astype(jnp.bfloat16), "seq").astype(jnp.float32),
        lax.psum(owned_grads[13].astype(jnp.bfloat16), "seq").astype(jnp.float32),
        lax.psum(owned_grads[14].astype(jnp.bfloat16), "seq").astype(jnp.float32),
    )
    return (output, grad_inputs.reshape(inputs.shape)) + tuple(summed)


def solution(mesh):
    placed = (
        P("dp", "seq", None),
        P("dp", None),
        P("dp", None),
        P("dp", None),
        P("dp"),
        P("dp"),
        P("dp", None),
        P("dp"),
        P("dp"),
        P("dp"),
        P("dp", None),
        P("dp"),
        P("dp", None),
        P("dp"),
        P("dp"),
        P("dp"),
        P("dp", "seq", None),
    )
    return jax.shard_map(
        local,
        mesh=mesh,
        in_specs=placed,
        out_specs=(
            P("dp", "seq", None),
            P("dp", "seq", None),
            P("dp", None),
            P("dp", None),
            P("dp", None),
            P("dp"),
            P("dp"),
            P("dp", None),
            P("dp"),
            P("dp"),
            P("dp"),
            P("dp", None),
            P("dp"),
            P("dp", None),
            P("dp"),
            P("dp"),
            P("dp"),
        ),
        check_vma=False,
    )
```

profile of v0, /device:TPU:0, one launch (start us, length us, event | category | flops | bytes accessed | tf_op | source)
XLA Modules:
  0.0 830.0 jit_solution(2075484790764947876)
XLA Ops:
  11.2 13.5 %all-gather = bf16[8,1,128]{2,1,0:T(2,128)(2,1)S(1)} all-gather(bf16[1,1,128]{2,1,0:T(2,128)(2,1)S(1)} %bitcast.204), channel_id=1, replica_groups=mesh['dp'=8,'seq'=4] {'dp'}, dimensions={0}, use_global_device_ids=true | all-gather | bytes 2304 | tf_op jit(solution)/shard_map/all_gather | solution.py:206
  24.7 16.8 %all-gather.16.cloned.1.call-done = bf16[1024,1024]{1,0:T(8,128)(2,1)} async-done(((bf16[128,1024]{1,0:T(8,128)(2,1)}), bf16[1024,1024]{1,0:T(8,128)(2,1)}) %all-gather.16.cloned.1.call-update) | async-done | bytes 2097168 | tf_op jit(solution)/shard_map/all_gather | solution.py:204
  41.5 2.6 add_convert_fusion.3
  45.5 3.6 all-to-all-start
  49.2 10.3 %all-gather.1 = bf16[8,1,128]{2,1,0:T(2,128)(2,1)S(1)} all-gather(bf16[1,1,128]{2,1,0:T(2,128)(2,1)S(1)} %bitcast.205), channel_id=1, replica_groups=mesh['dp'=8,'seq'=4] {'dp'}, dimensions={0}, use_global_device_ids=true | all-gather | bytes 2304 | tf_op jit(solution)/shard_map/all_gather | solution.py:205
  59.5 12.3 %all-gather.18.cloned.1.call-done = bf16[1024,1024]{1,0:T(8,128)(2,1)} async-done(((bf16[128,1024]{1,0:T(8,128)(2,1)}), bf16[1024,1024]{1,0:T(8,128)(2,1)}) %all-gather.18.cloned.1.call-update) | async-done | bytes 2097168 | tf_op jit(solution)/shard_map/all_gather | solution.py:202
  71.7 2.6 add_convert_fusion.2
  75.8 3.6 all-to-all-start.1
  79.4 22.6 %all-gather.20.cloned.1.call-done = bf16[1024,1024]{1,0:T(8,128)(2,1)} async-done(((bf16[128,1024]{1,0:T(8,128)(2,1)}), bf16[1024,1024]{1,0:T(8,128)(2,1)}) %all-gather.20.cloned.1.call-update) | async-done | bytes 2097168 | tf_op jit(solution)/shard_map/all_gather | solution.py:203
  102.0 2.8 convolution_convert_fusion.4
  106.2 3.9 all-to-all-start.2
  111.7 2.3 reshape.198
  115.1 9.1 %all-to-all-done.2 = bf16[3,128,1024]{1,0,2:T(4,128)(2,1)S(1)} async-done(((bf16[3,128,1024]{1,0,2:T(4,128)(2,1)}), bf16[3,128,1024]{1,0,2:T(4,128)(2,1)S(1)}, u32[]{:S(2)}, u32[]{:S(2)}) %all-to-all-start.2) | async-done | bytes 786464 | tf_op jit(solution)/shard_map/all_to_all | solution.py:150
  127.2 2.1 fusion
  129.3 2.4 copy-done
  131.7 2.8 fusion.20
  136.0 3.5 all-to-all-start.3
  139.5 10.5 %all-gather.6 = bf16[8,1,128]{2,1,0:T(2,128)(2,1)S(1)} all-gather(bf16[1,1,128]{2,1,0:T(2,128)(2,1)S(1)} %bitcast.206), channel_id=1, replica_groups=mesh['dp'=8,'seq'=4] {'dp'}, dimensions={0}, use_global_device_ids=true | all-gather | bytes 2304 | tf_op jit(solution)/shard_map/all_gather | solution.py:214
  150.0 12.9 %all-gather.5 = bf16[8,1,512]{2,1,0:T(2,128)(2,1)S(1)} all-gather(bf16[1,1,512]{2,1,0:T(2,128)(2,1)S(1)} %reshape.226), channel_id=1, replica_groups=mesh['dp'=8,'seq'=4] {'dp'}, dimensions={0}, use_global_device_ids=true | all-gather | bytes 9216 | tf_op jit(solution)/shard_map/all_gather | solution.py:212
  163.0 9.6 %all-gather.2 = bf16[8,1,128]{2,1,0:T(2,128)(2,1)S(1)} all-gather(bf16[1,1,128]{2,1,0:T(2,128)(2,1)S(1)} %bitcast.207), channel_id=1, replica_groups=mesh['dp'=8,'seq'=4] {'dp'}, dimensions={0}, use_global_device_ids=true | all-gather | bytes 2304 | tf_op jit(solution)/shard_map/all_gather | solution.py:208
  172.5 11.3 %all-gather.4 = bf16[8,1,128]{2,1,0:T(2,128)(2,1)S(1)} all-gather(bf16[1,1,128]{2,1,0:T(2,128)(2,1)S(1)} %bitcast.208), channel_id=1, replica_groups=mesh['dp'=8,'seq'=4] {'dp'}, dimensions={0}, use_global_device_ids=true | all-gather | bytes 2304 | tf_op jit(solution)/shard_map/all_gather | solution.py:210
  183.8 8.8 %all-gather.3 = bf16[8,1,128]{2,1,0:T(2,128)(2,1)S(1)} all-gather(bf16[1,1,128]{2,1,0:T(2,128)(2,1)S(1)} %bitcast.209), channel_id=1, replica_groups=mesh['dp'=8,'seq'=4] {'dp'}, dimensions={0}, use_global_device_ids=true | all-gather | bytes 2304 | tf_op jit(solution)/shard_map/all_gather | solution.py:209
  192.6 10.0 %all-gather.7 = bf16[8,1,128]{2,1,0:T(2,128)(2,1)S(1)} all-gather(bf16[1,1,128]{2,1,0:T(2,128)(2,1)S(1)} %bitcast.210), channel_id=1, replica_groups=mesh['dp'=8,'seq'=4] {'dp'}, dimensions={0}, use_global_device_ids=true | all-gather | bytes 2304 | tf_op jit(solution)/shard_map/all_gather | solution.py:215
  202.6 10.0 %all-gather.8 = bf16[8,1,128]{2,1,0:T(2,128)(2,1)S(1)} all-gather(bf16[1,1,128]{2,1,0:T(2,128)(2,1)S(1)} %bitcast.211), channel_id=1, replica_groups=mesh['dp'=8,'seq'=4] {'dp'}, dimensions={0}, use_global_device_ids=true | all-gather | bytes 2304 | tf_op jit(solution)/shard_map/all_gather | solution.py:216
  213.6 3.2 fusion.34
  217.1 20.7 %multiply_convert_fusion.1 = (bf16[384,4096]{1,0:T(8,128)(2,1)}, f32[384,4096]{1,0:T(8,128)}, f32[384,4096]{1,0:T(8,128)}) fusion(f32[4096]{0:T(1024)S(1)} %bitcast.187, bf16[1024,4096]{1,0:T(8,128)(2,1)} %all-gather.24.cloned.1.call-done, f32[384,1024]{1,0:T(8,128)S(1)} %get-tuple-element.130, f32[1024]{0:T(1024)S(1)} %bitcast.197, ...), kind=kOutput, calls=%fused_computation.15 | convolution fusion | flops 3327000576 | bytes 25717760 | tf_op jit(solution)/shard_map/dot_general | solution.py:11
  237.8 59.7 %all-gather.26.cloned.1.call-done = bf16[4096,1024]{1,0:T(8,128)(2,1)} async-done(((bf16[512,1024]{1,0:T(8,128)(2,1)}), bf16[4096,1024]{1,0:T(8,128)(2,1)}) %all-gather.26.cloned.1.call-update) | async-done | bytes 8388624 | tf_op jit(solution)/shard_map/all_gather | solution.py:213
  297.5 7.0 fusion.35
  307.3 13.3 %fusion.29 = (bf16[4096]{0:T(1024)(128)(2,1)S(1)}, bf16[384,4096]{1,0:T(8,128)(2,1)S(1)}) fusion(f32[384,4096]{1,0:T(8,128)} %get-tuple-element.125, f32[384,4096]{1,0:T(8,128)} %get-tuple-element.131, bf16[384,1024]{1,0:T(8,128)(2,1)S(1)} %get-tuple-element.115, bf16[4096,1024]{1,0:T(8,128)(2,1)} %all-gather.26.cloned.1.call-done), kind=kOutput, calls=%fused_computation.83 | convolution fusion | flops 3244814336 | bytes 24911872 | tf_op jit(solution)/shard_map/dot_general | solution.py:21
  320.6 3.9 multiply_reduce_fusion.2
  324.6 2.1 fusion.31
  330.3 3.7 all-to-all-start.4
  334.0 14.1 %all-to-all-done.4 = bf16[3,128,1024]{1,0,2:T(4,128)(2,1)S(1)} async-done(((bf16[3,128,1024]{1,0,2:T(4,128)(2,1)}), bf16[3,128,1024]{1,0,2:T(4,128)(2,1)S(1)}, u32[]{:S(2)}, u32[]{:S(2)}) %all-to-all-start.4) | async-done | bytes 786464 | tf_op jit(solution)/shard_map/all_to_all | solution.py:296
  351.4 6.5 multiply_reduce_fusion
  357.9 6.8 multiply_convert_fusion
  364.7 2.5 multiply_convert_fusion.3
  367.6 2.3 copy.88
  369.9 17.6 %all_to_all.140 = bf16[3,512,256]{2,0,1:T(4,128)(2,1)S(1)} all-to-all(bf16[3,512,256]{2,0,1:T(4,128)(2,1)} %copy.88), channel_id=1, replica_groups=mesh['dp'=8,'seq'=4] {'seq'}, dimensions={1} | all-to-all | bytes 1572864 | tf_op jit(solution)/shard_map/all_to_all | solution.py:299
  390.3 2.6 convert_bitcast_fusion.2
  392.9 3.9 copy.106
  396.9 5.7 multiply_convert_fusion.2
  402.6 2.3 copy.92
  404.9 16.0 %all_to_all.141 = bf16[3,512,256]{2,0,1:T(4,128)(2,1)S(1)} all-to-all(bf16[3,512,256]{2,0,1:T(4,128)(2,1)} %copy.92), channel_id=1, replica_groups=mesh['dp'=8,'seq'=4] {'seq'}, dimensions={1} | all-to-all | bytes 1572864 | tf_op jit(solution)/shard_map/all_to_all | solution.py:300
  421.8 2.6 convert_bitcast_fusion.1
  424.4 4.0 copy.108
  428.5 7.8 fusion.17
  437.9 13.4 %all_to_all.142 = bf16[3,512,256]{2,0,1:T(4,128)(2,1)S(1)} all-to-all(bf16[3,512,256]{2,0,1:T(4,128)(2,1)S(1)} %copy.96), channel_id=1, replica_groups=mesh['dp'=8,'seq'=4] {'seq'}, dimensions={1} | all-to-all | bytes 1572864 | tf_op jit(solution)/shard_map/all_to_all | solution.py:301
  453.1 2.6 convert_bitcast_fusion
  455.7 4.0 copy.110
  460.1 3.8 convolution_convert_fusion.2
  463.9 10.4 %convolution_convert_fusion.1 = bf16[1024,4096]{1,0:T(8,128)(2,1)} fusion(bf16[384,4096]{1,0:T(8,128)(2,1)} %copy-done.38, f32[384,1024]{1,0:T(8,128)} %copy-done.7, f32[1024]{0:T(1024)S(1)} %bitcast.199, f32[1024]{0:T(1024)S(1)} %bitcast.192, f32[384]{0:T(512)S(1)} %fusion.22, f32[384]{0:T(512)S(1)} %broadcast_multiply_fusion.1), kind=kOutput, calls=%fused_computation.10 | convolution fusion | flops 3227385856 | bytes 13118464 | tf_op jit(solution)/shard_map/dot_general | solution.py:15
  475.4 8.7 %convolution_convert_fusion = bf16[4096,1024]{1,0:T(8,128)(2,1)} fusion(bf16[384,4096]{1,0:T(8,128)(2,1)} %get-tuple-element.124, bf16[384,1024]{1,0:T(8,128)(2,1)S(1)} %copy-done.20), kind=kOutput, calls=%fused_computation.9 | convolution fusion | flops 3225419776 | bytes 12320768 | tf_op jit(solution)/shard_map/dot_general | solution.py:15
  487.9 15.7 %reduce-scatter.23.cloned.1.call-done = bf16[128,1024]{1,0:T(8,128)(2,1)} async-done(((bf16[1024,1024]{1,0:T(8,128)(2,1)}), bf16[128,1024]{1,0:T(8,128)(2,1)}) %reduce-scatter.23.cloned.1.call-update) | async-done | bytes 262160
  505.4 35.2 %reduce-scatter.13.cloned.1.call-done = bf16[128,1024]{1,0:T(8,128)(2,1)} async-done(((bf16[1024,1024]{1,0:T(8,128)(2,1)}), bf16[128,1024]{1,0:T(8,128)(2,1)}) %reduce-scatter.13.cloned.1.call-update) | async-done | bytes 262160 | tf_op jit(solution)/shard_map/reduce_scatter | solution.py:334
  540.6 90.6 %reduce-scatter.15.cloned.1.call-done = bf16[128,4096]{1,0:T(8,128)(2,1)} async-done(((bf16[1024,4096]{1,0:T(8,128)(2,1)}), bf16[128,4096]{1,0:T(8,128)(2,1)}) %reduce-scatter.15.cloned.1.call-update) | async-done | bytes 1048592 | tf_op jit(solution)/shard_map/reduce_scatter | solution.py:346
  631.2 90.1 %reduce-scatter.17.cloned.1.call-done = bf16[512,1024]{1,0:T(8,128)(2,1)} async-done(((bf16[4096,1024]{1,0:T(8,128)(2,1)}), bf16[512,1024]{1,0:T(8,128)(2,1)}) %reduce-scatter.17.cloned.1.call-update) | async-done | bytes 1048592 | tf_op jit(solution)/shard_map/reduce_scatter | solution.py:352
  724.8 26.1 %all-reduce.9 = (bf16[1024]{0:T(1024)(128)(2,1)S(1)}, bf16[1024]{0:T(1024)(128)(2,1)S(1)}, bf16[1024]{0:T(1024)(128)(2,1)S(1)}, bf16[1024]{0:T(1024)(128)(2,1)S(...) all-reduce(bf16[1024]{0:T(1024)(128)(2,1)S(1)} %bitcast.195, ...), channel_id=5, replica_groups=mesh['dp'=8,'seq'=4] {'dp'}, use_global_device_ids=true, to_apply=%region_18.0.clone | all-reduce | flops 12288 | bytes 49152
  751.6 10.5 %all-reduce.10 = (bf16[128]{0:T(256)(128)(2,1)S(1)}, bf16[128]{0:T(256)(128)(2,1)S(1)}, bf16[128]{0:T(256)(128)(2,1)S(1)}, bf16[128]{0:T(256)(128)(2,1)S(1)}, bf...) all-reduce(bf16[128]{0:T(256)(128)(2,1)S(1)} %dynamic-slice.1, ...), channel_id=1, replica_groups=mesh['dp'=8,'seq'=4] {'seq'}, use_global_device_ids=true, to_apply=%region_19.0 | all-reduce | flops 1536 | bytes 6144 | tf_op jit(solution)/shard_map/psum | solution.py:369
  766.9 2.9 fusion.37
  771.7 2.3 add_add_fusion.2
  774.0 38.3 %all-reduce.14.cloned.1.call-done = (bf16[128,1024]{0,1:T(8,128)(2,1)}, bf16[128,1024]{0,1:T(8,128)(2,1)}, bf16[128,1024]{0,1:T(8,128)(2,1)}, bf16[128,1024]{1,0...) async-done(((bf16[128,1024]{0,1:T(8,128)(2,1)}, bf16[128,1024]{0,1:T(8,128)(2,1)}, bf16[128,1024]{0,1:T(8,128)(2,1)}, bf16[128,1024]{1,0:T(8,128)(2,1)}, ...) | async-done | bytes 3145744 | tf_op jit(solution)/shard_map/psum | solution.py:366
  812.3 2.0 copy.99
  814.3 1.9 copy.100
  816.2 1.9 copy.101
  (198 shorter events, 54.9 us)
Async XLA Ops:
  7.2 4.0 copy-start.23
  7.2 34.3 %copy-start.33 = (bf16[3,128,1024]{2,1,0:T(8,128)(2,1)S(1)}, bf16[3,128,1024]{2,1,0:T(8,128)(2,1)}, u32[]{:S(2)}) copy-start(bf16[3,128,1024]{2,1,0:T(8,128)(2,1)} %param.17) | copy-start | bytes 2359300
  7.2 34.3 %all-gather.16.cloned.1.call-start = ((), (), s32[]{:S(2)}) async-start(), calls=%async_computation.14 | async-start | bytes 2359296 | tf_op jit(solution)/shard_map/all_gather | solution.py:204
  7.9 63.8 %all-gather.18.cloned.1.call-start = ((), (), s32[]{:S(2)}) async-start(), calls=%async_computation.15 | async-start | bytes 2359296 | tf_op jit(solution)/shard_map/all_gather | solution.py:202
  8.7 93.3 %all-gather.20.cloned.1.call-start = ((), (), s32[]{:S(2)}) async-start(), calls=%async_computation.16 | async-start | bytes 2359296 | tf_op jit(solution)/shard_map/all_gather | solution.py:203
  9.4 204.1 %all-gather.22.cloned.1.call-start = ((), (), s32[]{:S(2)}) async-start(), calls=%async_computation.17 | async-start | bytes 2359296 | tf_op jit(solution)/shard_map/all_gather | solution.py:207
  10.0 207.1 %all-gather.24.cloned.1.call-start = ((), (), s32[]{:S(2)}) async-start(), calls=%async_computation.18 | async-start | bytes 9437184 | tf_op jit(solution)/shard_map/all_gather | solution.py:211
  10.6 286.9 %all-gather.26.cloned.1.call-start = ((), (), s32[]{:S(2)}) async-start(), calls=%async_computation.19 | async-start | bytes 9437184 | tf_op jit(solution)/shard_map/all_gather | solution.py:213
  44.1 5.1 copy-start.24
  45.5 30.2 %all-to-all-start = ((bf16[3,128,1024]{1,0,2:T(4,128)(2,1)}), bf16[3,128,1024]{1,0,2:T(4,128)(2,1)S(1)}, u32[]{:S(2)}, u32[]{:S(2)}) async-start(bf16[3,128,1024]{1,0,2:T(4,128)(2,1)} %copy.75), calls=%async_computation | async-start | bytes 2097152 | tf_op jit(solution)/shard_map/all_to_all | solution.py:151
  75.8 30.5 %all-to-all-start.1 = ((bf16[3,128,1024]{1,0,2:T(4,128)(2,1)}), bf16[3,128,1024]{1,0,2:T(4,128)(2,1)S(1)}, u32[]{:S(2)}, u32[]{:S(2)}) async-start(bf16[3,128,1024]{1,0,2:T(4,128)(2,1)} %copy.77), calls=%async_computation.1 | async-start | bytes 2097152 | tf_op jit(solution)/shard_map/all_to_all | solution.py:149
  106.2 18.0 %all-to-all-start.2 = ((bf16[3,128,1024]{1,0,2:T(4,128)(2,1)}), bf16[3,128,1024]{1,0,2:T(4,128)(2,1)S(1)}, u32[]{:S(2)}, u32[]{:S(2)}) async-start(bf16[3,128,1024]{1,0,2:T(4,128)(2,1)} %copy.79), calls=%async_computation.2 | async-start | bytes 2097152 | tf_op jit(solution)/shard_map/all_to_all | solution.py:150
  125.3 1.9 copy-start.5
  127.2 4.5 copy-start
  127.2 4.5 copy-start.8
  134.5 5.0 copy-start.25
  134.5 15.5 %copy-start.22 = (bf16[512]{0:T(512)(128)(2,1)S(1)}, bf16[512]{0:T(512)(128)(2,1)}, u32[]{:S(2)}) copy-start(bf16[512]{0:T(512)(128)(2,1)} %param.28) | copy-start | bytes 3076
  134.6 28.4 %copy-start.26 = (bf16[128]{0:T(256)(128)(2,1)S(1)}, bf16[128]{0:T(256)(128)(2,1)}, u32[]{:S(2)}) copy-start(bf16[128]{0:T(256)(128)(2,1)} %param.24) | copy-start | bytes 772
  134.6 38.0 %copy-start.27 = (bf16[128]{0:T(256)(128)(2,1)S(1)}, bf16[128]{0:T(256)(128)(2,1)}, u32[]{:S(2)}) copy-start(bf16[128]{0:T(256)(128)(2,1)} %param.26) | copy-start | bytes 772
  134.6 49.2 %copy-start.28 = (bf16[128]{0:T(256)(128)(2,1)S(1)}, bf16[128]{0:T(256)(128)(2,1)}, u32[]{:S(2)}) copy-start(bf16[128]{0:T(256)(128)(2,1)} %param.25) | copy-start | bytes 772
  134.6 58.0 %copy-start.29 = (bf16[128]{0:T(256)(128)(2,1)S(1)}, bf16[128]{0:T(256)(128)(2,1)}, u32[]{:S(2)}) copy-start(bf16[128]{0:T(256)(128)(2,1)} %param.31) | copy-start | bytes 772
  134.6 68.0 %copy-start.30 = (bf16[128]{0:T(256)(128)(2,1)S(1)}, bf16[128]{0:T(256)(128)(2,1)}, u32[]{:S(2)}) copy-start(bf16[128]{0:T(256)(128)(2,1)} %param.32) | copy-start | bytes 772
  136.0 76.6 %all-to-all-start.3 = ((bf16[3,512,256]{2,0,1:T(4,128)(2,1)}), bf16[3,512,256]{2,0,1:T(4,128)(2,1)S(1)}, u32[]{:S(2)}, u32[]{:S(2)}) async-start(bf16[3,512,256]{2,0,1:T(4,128)(2,1)} %copy.82), calls=%async_computation.3 | async-start | bytes 2097152 | tf_op jit(solution)/shard_map/all_to_all | solution.py:154
  213.5 3.2 copy-start.17
  216.7 103.9 %copy-start.7 = (f32[384,1024]{1,0:T(8,128)}, f32[384,1024]{1,0:T(8,128)S(1)}, u32[]{:S(2)}) copy-start(f32[384,1024]{1,0:T(8,128)S(1)} %get-tuple-element.130) | copy-start | bytes 4718596
  297.5 7.4 copy-start.4
  305.5 15.1 %slice-start = ((s8[8388608]{0:T(1024)(128)(4,1)}), s8[4194304]{0:T(1024)(128)(4,1)S(1)}, s32[]{:S(2)}) async-start(s8[8388608]{0:T(1024)(128)(4,1)} %bitcast.212), calls=%async_computation.27 | async-start | bytes 8388608
  307.3 13.3 %copy-start.19 = (bf16[384,1024]{1,0:T(8,128)(2,1)}, bf16[384,1024]{1,0:T(8,128)(2,1)S(1)}, u32[]{:S(2)}) copy-start(bf16[384,1024]{1,0:T(8,128)(2,1)S(1)} %get-tuple-element.115) | copy-start | bytes 2359300
  307.3 13.3 %slice-start.1 = ((s8[8388608]{0:T(1024)(128)(4,1)}), s8[4194304]{0:T(1024)(128)(4,1)S(1)}, s32[]{:S(2)}) async-start(s8[8388608]{0:T(1024)(128)(4,1)} %bitcast.212), calls=%async_computation.28 | async-start | bytes 8388608
  320.6 4.0 copy-start.38
  324.6 3.2 copy-start.32
  326.9 0.9 copy-start.21
  330.3 17.8 %all-to-all-start.4 = ((bf16[3,128,1024]{1,0,2:T(4,128)(2,1)}), bf16[3,128,1024]{1,0,2:T(4,128)(2,1)S(1)}, u32[]{:S(2)}, u32[]{:S(2)}) async-start(bf16[3,128,1024]{1,0,2:T(4,128)(2,1)} %copy.85), calls=%async_computation.4 | async-start | bytes 2097152 | tf_op jit(solution)/shard_map/all_to_all | solution.py:296
  333.9 150.3 %reduce-scatter.19.cloned.1.call-start = ((), (), s32[]{:S(2)}) async-start(), calls=%async_computation.23 | async-start | bytes 2359296
  357.9 6.8 copy-start.6
  364.7 2.9 copy-start.1
  369.9 20.4 %copy-start.34 = (bf16[3,128,1024]{2,1,0:T(8,128)(2,1)S(1)}, bf16[3,128,1024]{2,1,0:T(8,128)(2,1)}, u32[]{:S(2)}) copy-start(bf16[3,128,1024]{2,1,0:T(8,128)(2,1)} %param.17) | copy-start | bytes 2359300
  387.7 0.9 copy-start.2
  389.4 0.9 copy-start.14
  396.9 89.2 %reduce-scatter.21.cloned.1.call-start = ((), (), s32[]{:S(2)}) async-start(), calls=%async_computation.24 | async-start | bytes 2359296
  404.9 16.9 %copy-start.35 = (bf16[3,128,1024]{2,1,0:T(8,128)(2,1)S(1)}, bf16[3,128,1024]{2,1,0:T(8,128)(2,1)}, u32[]{:S(2)}) copy-start(bf16[3,128,1024]{2,1,0:T(8,128)(2,1)} %param.17) | copy-start | bytes 2359300
  421.8 2.6 copy-start.16
  428.4 75.2 %reduce-scatter.23.cloned.1.call-start = ((), (), s32[]{:S(2)}) async-start(), calls=%async_computation.25 | async-start | bytes 2359296
  437.9 15.2 %copy-start.36 = (bf16[3,128,1024]{2,1,0:T(8,128)(2,1)S(1)}, bf16[3,128,1024]{2,1,0:T(8,128)(2,1)}, u32[]{:S(2)}) copy-start(bf16[3,128,1024]{2,1,0:T(8,128)(2,1)} %param.17) | copy-start | bytes 2359300
  452.2 0.9 copy-start.9
  455.7 4.3 copy-start.18
  459.8 80.9 %reduce-scatter.13.cloned.1.call-start = ((), (), s32[]{:S(2)}) async-start(), calls=%async_computation.20 | async-start | bytes 2359296 | tf_op jit(solution)/shard_map/reduce_scatter | solution.py:334
  463.9 167.3 %reduce-scatter.15.cloned.1.call-start = ((), (), s32[]{:S(2)}) async-start(), calls=%async_computation.21 | async-start | bytes 9437184 | tf_op jit(solution)/shard_map/reduce_scatter | solution.py:346
  474.3 1.1 copy-start.20
  474.3 247.0 %reduce-scatter.17.cloned.1.call-start = ((), (), s32[]{:S(2)}) async-start(), calls=%async_computation.22 | async-start | bytes 9437184 | tf_op jit(solution)/shard_map/reduce_scatter | solution.py:352
  484.1 238.5 %copy-start.37 = (u32[32]{0:T(128)S(1)}, u32[32]{0:T(128)}, u32[]{:S(2)}) copy-start(u32[32]{0:T(128)} %constant.93) | copy-start | bytes 388
  484.1 240.4 %copy-start.3 = (bf16[3,512,256]{2,1,0:T(8,128)(2,1)S(1)}, bf16[3,512,256]{2,1,0:T(8,128)(2,1)}, u32[]{:S(2)}) copy-start(bf16[3,512,256]{2,1,0:T(8,128)(2,1)} %copy-done.2) | copy-start | bytes 2359300
  484.1 328.1 %all-reduce.14.cloned.1.call-start = ((), (), s32[]{:S(2)}) async-start(), calls=%async_computation.26 | async-start | bytes 6291456 | tf_op jit(solution)/shard_map/psum | solution.py:366
  724.7 45.1 %copy-start.15 = (bf16[48,8,4,256]{3,1,2,0:T(8,128)(2,1)S(1)}, bf16[48,8,4,256]{3,1,2,0:T(8,128)(2,1)}, u32[]{:S(2)}) copy-start(bf16[48,8,4,256]{3,1,2,0:T(8,128)(2,1)} %copy-done.14) | copy-start | bytes 2359300
  762.2 7.6 copy-start.31
  769.8 1.1 copy-start.10
  769.8 1.8 copy-start.11
  812.2 7.6 copy-start.13
  812.3 9.1 %copy-start.12 = (bf16[512,1024]{1,0:T(8,128)(2,1)S(1)}, bf16[512,1024]{1,0:T(8,128)(2,1)}, u32[]{:S(2)}) copy-start(bf16[512,1024]{1,0:T(8,128)(2,1)} %get-tuple-element.113) | copy-start | bytes 3145732
Sparse Core Ops, SparseCore 0:
  9.6 31.7 all-gather.15
  43.1 28.6 all-gather.17
  73.3 28.5 all-gather.19
  103.4 28.5 all-gather.21
  133.5 81.7 all-gather.23
  216.7 80.6 all-gather.25
  397.0 32.8 reduce-scatter.18
  432.2 34.4 reduce-scatter.20
  469.0 34.5 reduce-scatter.22
  506.3 34.2 reduce-scatter.12
  542.9 88.2 reduce-scatter.14
  633.4 87.9 reduce-scatter.16
  725.6 86.5 all-reduce.13
where the time goes:
time: 835 us; the launch traced here: 830 us
  waiting for transfers between devices  408 us (49%)
  blocking collectives  180 us (22%)
  matrix products  121 us (14%)
  local copies, waits for them, and re-layouts  59 us (7%)
  other arithmetic  25.5 us (3%)
  starting transfers between devices  19.1 us (2%)
  between operations  16.5 us (2%)
    reduce_scatter x1, waiting for transfers between devices, local(): lax.psum_scatter(grad_w_up.astype(jnp.bfloat16), 'dp', scatter_dimension=...  90.6 us
    reduce_scatter x1, waiting for transfers between devices, local(): lax.psum_scatter(grad_w_down.astype(jnp.bfloat16), 'dp', scatter_dimensio...  90.1 us
    all_gather x1, waiting for transfers between devices, local(): lax.all_gather(w_down, 'dp', axis=0, tiled=True)  59.7 us
    dot_general x6, matrix products, dot_rows(): return jnp.dot(former, latter, preferred_element_type=jnp.float32)  38.9 us
    psum x1, waiting for transfers between devices, local(): lax.psum(owned_grads[0].astype(jnp.bfloat16), 'seq').astype(jnp.float32)  38.3 us
    reduce_scatter x1, waiting for transfers between devices, local(): lax.psum_scatter(grad_w_out.astype(jnp.bfloat16), 'dp', scatter_dimension...  35.2 us
    unnamed x108, local copies, waits for them, and re-layouts  33.4 us
    dot_general x6, matrix products, dot_left(): lax.dot_general(former, latter, (((0,), (0,)), ((), ())), preferred_eleme...  30.7 us
  transfers between devices with their start and end apart: 18, of which 11 were waited for; matrix products, arithmetic and copies ran while one was open for 15% of the time, Pallas kernels for 0%

commit v1 on v0

--- a/solution.py
+++ b/solution.py
@@ -5,6 +5,31 @@
 
 HEAD_DIM = 64
 EPSILON = 1e-12
+
+
+def proceed_series_all(my_data, dim_i):
+    upper = list(my_data.shape[1:])
+    upper[dim_i] *= my_data.shape[0]
+    return jnp.moveaxis(my_data, 0, dim_i).reshape(upper)
+
+
+def perform_halves(work_x, shard_axis):
+    local_now, answer = (lax.axis_size(shard_axis), lax.axis_index(shard_axis))
+    piece_out, outer = (work_x[None], 1)
+    while outer < local_now:
+        now = lax.ppermute(
+            piece_out, shard_axis, [(dev_j, dev_j ^ outer) for dev_j in range(local_now)]
+        )
+        seen_now = answer & outer == 0
+        piece_out = jnp.concatenate(
+            [jnp.where(seen_now, piece_out, now), jnp.where(seen_now, now, piece_out)]
+        )
+        outer *= 2
+    return piece_out
+
+
+def wrap_seats_all(array_in, frame, dim_k):
+    return proceed_series_all(perform_halves(array_in, frame), dim_k)
 
 
 def dot_rows(former, latter):
@@ -210,7 +235,7 @@
         lax.all_gather(shift_one, "dp", axis=0, tiled=True),
         lax.all_gather(w_up, "dp", axis=0, tiled=True),
         lax.all_gather(b_up, "dp", axis=0, tiled=True),
-        lax.all_gather(w_down, "dp", axis=0, tiled=True),
+        wrap_seats_all(w_down, "dp", 0),
         lax.all_gather(b_down, "dp", axis=0, tiled=True),
         lax.all_gather(gain_two, "dp", axis=0, tiled=True),
         lax.all_gather(shift_two, "dp", axis=0, tiled=True),

time: 835 us -> 1100 us (1.32)
  blocking collectives: 180 us -> 515 us
  waiting for transfers between devices: 408 us -> 292 us
  other arithmetic: 25.5 us -> 53.4 us
  matrix products: 121 us -> 133 us
    all_gather x1, blocking collectives: 8.8 us -> 227 us  [local(): lax.all_gather(gain_one, 'dp', axis=0, tiled=True)]
    all_gather x1, blocking collectives: 10.3 us -> 85.6 us  [local(): lax.all_gather(b_query, 'dp', axis=0, tiled=True)]
    all_gather x1, waiting for transfers between devices: 59.7 us -> 0.01 us  [local(): lax.all_gather(w_down, 'dp', axis=0, tiled=True)]
    all_gather x1, blocking collectives: 9.57 us -> 61.5 us  [local(): lax.all_gather(b_out, 'dp', axis=0, tiled=True)]
    all_gather x1, waiting for transfers between devices: 22.6 us -> 0.01 us  [local(): lax.all_gather(w_key, 'dp', axis=0, tiled=True)]
    all_gather x1, waiting for transfers between devices: 16.8 us -> 0.01 us  [local(): lax.all_gather(w_value, 'dp', axis=0, tiled=True)]
    concatenate x0 -> x3, other arithmetic: none -> 13.2 us  [perform_halves(): jnp.concatenate([jnp.where(seen_now, piece_out, now), jnp.where(seen_now,...]
    all_gather x1, waiting for transfers between devices: 12.3 us -> 0.01 us  [local(): lax.all_gather(w_query, 'dp', axis=0, tiled=True)]
  transfers between devices with their start and end apart: 18 -> 21, of which waited for: 11 -> 9; matrix products, arithmetic and copies ran while one was open for 15% -> 17% of each run, Pallas kernels for 0% -> 0%
where the time goes in v1:
time: 1100 us
  blocking collectives  515 us (47%)
  waiting for transfers between devices  292 us (27%)
  matrix products  133 us (12%)
  local copies, waits for them, and re-layouts  64.6 us (6%)
  other arithmetic  53.4 us (5%)
  starting transfers between devices  24.6 us (2%)
  between operations  16.2 us (1%)
    all_gather x1, blocking collectives, local(): lax.all_gather(gain_one, 'dp', axis=0, tiled=True)  227 us
    reduce_scatter x1, waiting for transfers between devices, local(): lax.psum_scatter(grad_w_up.astype(jnp.bfloat16), 'dp', scatter_dimension=...  90.5 us
    reduce_scatter x1, waiting for transfers between devices, local(): lax.psum_scatter(grad_w_down.astype(jnp.bfloat16), 'dp', scatter_dimensio...  90.2 us
    all_gather x1, blocking collectives, local(): lax.all_gather(b_query, 'dp', axis=0, tiled=True)  85.6 us
    all_gather x1, blocking collectives, local(): lax.all_gather(b_out, 'dp', axis=0, tiled=True)  61.5 us
    dot_general x7, matrix products, dot_rows(): return jnp.dot(former, latter, preferred_element_type=jnp.float32)  43.7 us
    psum x1, waiting for transfers between devices, local(): lax.psum(owned_grads[0].astype(jnp.bfloat16), 'seq').astype(jnp.float32)  38.4 us
    reduce_scatter x1, waiting for transfers between devices, local(): lax.psum_scatter(grad_w_out.astype(jnp.bfloat16), 'dp', scatter_dimension...  35.4 us
  transfers between devices with their start and end apart: 21, of which 9 were waited for; matrix products, arithmetic and copies ran while one was open for 17% of the time, Pallas kernels for 0%

profile of v1, /device:TPU:0, one launch (start us, length us, event | category | flops | bytes accessed | tf_op | source)
XLA Modules:
  0.0 1098.6 jit_solution(296451868258220752)
XLA Ops:
  11.1 2.5 collective-permute-done
  17.5 2.9 collective-permute-start.1
  20.5 85.6 %all-gather.1 = bf16[8,1,128]{2,1,0:T(2,128)(2,1)S(1)} all-gather(bf16[1,1,128]{2,1,0:T(2,128)(2,1)S(1)} %bitcast.213), channel_id=1, replica_groups=mesh['dp'=8,'seq'=4] {'dp'}, dimensions={0}, use_global_device_ids=true | all-gather | bytes 2304 | tf_op jit(solution)/shard_map/all_gather | solution.py:230
  106.1 2.6 add_convert_fusion.2
  110.1 3.7 all-to-all-start.1
  113.7 8.6 all-gather
  122.4 2.9 convolution_convert_fusion.4
  128.0 4.2 all-to-all-start.2
  132.2 3.5 broadcast_select_fusion.3
  135.7 2.8 add_convert_fusion.3
  139.9 5.8 all-to-all-done.2
  145.8 4.5 all-to-all-start
  150.3 4.1 pad_maximum_fusion.1
  157.7 3.1 copy.123
  160.8 2.3 reshape.217
  163.2 7.5 multiply_reduce_fusion.1
  170.7 2.8 copy.125
  175.2 7.0 fusion
  183.6 3.6 fusion.20
  187.3 2.4 copy.82
  189.7 4.2 all-to-all-start.3
  193.9 61.5 %all-gather.2 = bf16[8,1,128]{2,1,0:T(2,128)(2,1)S(1)} all-gather(bf16[1,1,128]{2,1,0:T(2,128)(2,1)S(1)} %bitcast.215), channel_id=1, replica_groups=mesh['dp'=8,'seq'=4] {'dp'}, dimensions={0}, use_global_device_ids=true | all-gather | bytes 2304 | tf_op jit(solution)/shard_map/all_gather | solution.py:233
  255.4 226.6 %all-gather.3 = bf16[8,1,128]{2,1,0:T(2,128)(2,1)S(1)} all-gather(bf16[1,1,128]{2,1,0:T(2,128)(2,1)S(1)} %bitcast.216), channel_id=1, replica_groups=mesh['dp'=8,'seq'=4] {'dp'}, dimensions={0}, use_global_device_ids=true | all-gather | bytes 2304 | tf_op jit(solution)/shard_map/all_gather | solution.py:234
  482.0 8.6 all-gather.4
  490.7 12.7 %all-gather.5 = bf16[8,1,512]{2,1,0:T(2,128)(2,1)S(1)} all-gather(bf16[1,1,512]{2,1,0:T(2,128)(2,1)S(1)} %reshape.242), channel_id=1, replica_groups=mesh['dp'=8,'seq'=4] {'dp'}, dimensions={0}, use_global_device_ids=true | all-gather | bytes 9216 | tf_op jit(solution)/shard_map/all_gather | solution.py:237
  503.4 9.1 all-gather.6
  512.6 9.6 all-gather.7
  522.1 9.1 all-gather.8
  532.2 3.1 fusion.34
  536.8 5.7 broadcast_select_fusion.1
  542.5 7.6 pad_maximum_fusion
  550.1 21.6 %multiply_convert_fusion.1 = (bf16[384,4096]{1,0:T(8,128)(2,1)S(1)}, f32[384,4096]{1,0:T(8,128)}, f32[384,4096]{1,0:T(8,128)}) fusion(f32[4096]{0:T(1024)S(1)} %bitcast.192, bf16[1024,4096]{1,0:T(8,128)(2,1)} %all-gather.24.cloned.1.call-done, f32[384,1024]{1,0:T(8,128)S(1)} %copy-done.12, f32[1024]{0:T(1024)S(1)} %bitcast.204, f32[1024]{0:T(1024)S(1)} %bitcast.193, ...), kind=kOutput, calls=%fused_computation.16 | convolution fusion | flops 3327000576 | bytes 25717760 | tf_op jit(solution)/shard_map/dot_general | solution.py:36
  571.8 3.6 fusion.36
  576.5 7.0 fusion.35
  586.9 13.3 %fusion.29 = (bf16[4096]{0:T(1024)(128)(2,1)S(1)}, bf16[384,4096]{1,0:T(8,128)(2,1)S(1)}) fusion(f32[384,4096]{1,0:T(8,128)} %get-tuple-element.125, f32[384,4096]{1,0:T(8,128)} %get-tuple-element.137, bf16[384,1024]{1,0:T(8,128)(2,1)S(1)} %get-tuple-element.115, bf16[4096,1024]{1,0:T(8,128)(2,1)} %all-gather.26.cloned.1.call-done), kind=kOutput, calls=%fused_computation.96 | convolution fusion | flops 3244814336 | bytes 24911872 | tf_op jit(solution)/shard_map/dot_general | solution.py:46
  600.2 4.0 multiply_reduce_fusion.2
  608.4 4.0 all-to-all-start.4
  612.3 14.1 %all-to-all-done.4 = bf16[3,128,1024]{1,0,2:T(4,128)(2,1)S(1)} async-done(((bf16[3,128,1024]{1,0,2:T(4,128)(2,1)}), bf16[3,128,1024]{1,0,2:T(4,128)(2,1)S(1)}, u32[]{:S(2)}, u32[]{:S(2)}) %all-to-all-start.4) | async-done | bytes 786464 | tf_op jit(solution)/shard_map/all_to_all | solution.py:321
  627.5 7.7 fusion.17
  636.8 16.5 %all_to_all.140 = bf16[3,512,256]{2,0,1:T(4,128)(2,1)S(1)} all-to-all(bf16[3,512,256]{2,0,1:T(4,128)(2,1)S(1)} %copy.96), channel_id=1, replica_groups=mesh['dp'=8,'seq'=4] {'seq'}, dimensions={1} | all-to-all | bytes 1572864 | tf_op jit(solution)/shard_map/all_to_all | solution.py:326
  655.2 2.6 convert_bitcast_fusion
  657.8 3.9 copy.110
  661.8 6.7 multiply_reduce_fusion
  668.5 6.9 multiply_convert_fusion
  675.4 2.5 multiply_convert_fusion.3
  680.7 15.6 %all_to_all.141 = bf16[3,512,256]{2,0,1:T(4,128)(2,1)S(1)} all-to-all(bf16[3,512,256]{2,0,1:T(4,128)(2,1)} %copy.88), channel_id=1, replica_groups=mesh['dp'=8,'seq'=4] {'seq'}, dimensions={1} | all-to-all | bytes 1572864 | tf_op jit(solution)/shard_map/all_to_all | solution.py:324
  698.1 2.6 convert_bitcast_fusion.2
  700.8 4.0 copy.106
  704.9 5.8 multiply_convert_fusion.2
  712.9 14.8 %all_to_all.142 = bf16[3,512,256]{2,0,1:T(4,128)(2,1)S(1)} all-to-all(bf16[3,512,256]{2,0,1:T(4,128)(2,1)} %copy.92), channel_id=1, replica_groups=mesh['dp'=8,'seq'=4] {'seq'}, dimensions={1} | all-to-all | bytes 1572864 | tf_op jit(solution)/shard_map/all_to_all | solution.py:325
  729.6 2.6 convert_bitcast_fusion.1
  732.2 4.0 copy.108
  736.3 3.8 convolution_convert_fusion.2
  740.1 10.3 convolution_convert_fusion.1
  751.6 8.7 convolution_convert_fusion
  764.1 10.9 reduce-scatter.21.cloned.1.call-done
  776.8 35.4 %reduce-scatter.13.cloned.1.call-done = bf16[128,1024]{1,0:T(8,128)(2,1)} async-done(((bf16[1024,1024]{1,0:T(8,128)(2,1)}), bf16[128,1024]{1,0:T(8,128)(2,1)}) %reduce-scatter.13.cloned.1.call-update) | async-done | bytes 262160 | tf_op jit(solution)/shard_map/reduce_scatter | solution.py:359
  812.2 90.5 %reduce-scatter.15.cloned.1.call-done = bf16[128,4096]{1,0:T(8,128)(2,1)} async-done(((bf16[1024,4096]{1,0:T(8,128)(2,1)}), bf16[128,4096]{1,0:T(8,128)(2,1)}) %reduce-scatter.15.cloned.1.call-update) | async-done | bytes 1048592 | tf_op jit(solution)/shard_map/reduce_scatter | solution.py:371
  902.7 90.2 %reduce-scatter.17.cloned.1.call-done = bf16[512,1024]{1,0:T(8,128)(2,1)} async-done(((bf16[4096,1024]{1,0:T(8,128)(2,1)}), bf16[512,1024]{1,0:T(8,128)(2,1)}) %reduce-scatter.17.cloned.1.call-update) | async-done | bytes 1048592 | tf_op jit(solution)/shard_map/reduce_scatter | solution.py:377
  996.4 26.1 %all-reduce.9 = (bf16[1024]{0:T(1024)(128)(2,1)S(1)}, bf16[1024]{0:T(1024)(128)(2,1)S(1)}, bf16[1024]{0:T(1024)(128)(2,1)S(1)}, bf16[1024]{0:T(1024)(128)(2,1)S(...) all-reduce(bf16[1024]{0:T(1024)(128)(2,1)S(1)} %bitcast.203, ...), channel_id=5, replica_groups=mesh['dp'=8,'seq'=4] {'dp'}, use_global_device_ids=true, to_apply=%region_20.21.clone | all-reduce | flops 12288 | bytes 49152
  1023.2 10.4 all-reduce.10
  1038.2 2.9 fusion.37
  1045.3 38.4 %all-reduce.14.cloned.1.call-done = (bf16[128,1024]{0,1:T(8,128)(2,1)}, bf16[128,1024]{0,1:T(8,128)(2,1)}, bf16[128,1024]{0,1:T(8,128)(2,1)}, bf16[128,1024]{1,0...) async-done(((bf16[128,1024]{0,1:T(8,128)(2,1)}, bf16[128,1024]{0,1:T(8,128)(2,1)}, bf16[128,1024]{0,1:T(8,128)(2,1)}, bf16[128,1024]{1,0:T(8,128)(2,1)}, ...) | async-done | bytes 3145744 | tf_op jit(solution)/shard_map/psum | solution.py:391
  1083.8 2.9 convert_element_type.291
  (240 shorter events, 67.6 us)
Async XLA Ops:
  7.2 98.9 %all-gather.18.cloned.1.call-start = ((), (), s32[]{:S(2)}) async-start(), calls=%async_computation.15 | async-start | bytes 2359296 | tf_op jit(solution)/shard_map/all_gather | solution.py:227
  7.9 114.5 %all-gather.20.cloned.1.call-start = ((), (), s32[]{:S(2)}) async-start(), calls=%async_computation.16 | async-start | bytes 2359296 | tf_op jit(solution)/shard_map/all_gather | solution.py:228
  8.7 127.0 %all-gather.16.cloned.1.call-start = ((), (), s32[]{:S(2)}) async-start(), calls=%async_computation.14 | async-start | bytes 2359296 | tf_op jit(solution)/shard_map/all_gather | solution.py:229
  9.4 522.8 %all-gather.22.cloned.1.call-start = ((), (), s32[]{:S(2)}) async-start(), calls=%async_computation.17 | async-start | bytes 2359296 | tf_op jit(solution)/shard_map/all_gather | solution.py:232
  10.0 540.1 %all-gather.24.cloned.1.call-start = ((), (), s32[]{:S(2)}) async-start(), calls=%async_computation.18 | async-start | bytes 9437184 | tf_op jit(solution)/shard_map/all_gather | solution.py:236
  10.6 565.9 %all-gather.26.cloned.1.call-start = ((), (), s32[]{:S(2)}) async-start(), calls=%async_computation.19 | async-start | bytes 9437184 | tf_op jit(solution)/shard_map/all_gather | solution.py:257
  10.6 3.0 collective-permute-start
  15.0 5.4 copy-start.35
  15.0 91.0 %copy-start.45 = (bf16[3,128,1024]{2,1,0:T(8,128)(2,1)S(1)}, bf16[3,128,1024]{2,1,0:T(8,128)(2,1)}, u32[]{:S(2)}) copy-start(bf16[3,128,1024]{2,1,0:T(8,128)(2,1)} %param.17) | copy-start | bytes 2359300
  17.5 114.7 %collective-permute-start.1 = (bf16[2,512,1024]{2,1,0:T(8,128)(2,1)}, bf16[2,512,1024]{2,1,0:T(8,128)(2,1)}, u32[]{:S(2)}, u32[]{:S(2)}) collective-permute-start(bf16[2,512,1024]{2,1,0:T(8,128)(2,1)} %pad_maximum_fusion.2), channel_id=1, source_target_pairs={{0,8},{4,12},{8,0},{12,4},{16,24},{20,28},{24,16},{28,20},{1,9},{5... | collective-permute-start | bytes 6291464 | tf_op jit(solution)/shard_map/ppermute | solution.py:20
  108.7 5.1 copy-start.36
  110.1 17.9 %all-to-all-start.1 = ((bf16[3,128,1024]{1,0,2:T(4,128)(2,1)}), bf16[3,128,1024]{1,0,2:T(4,128)(2,1)S(1)}, u32[]{:S(2)}, u32[]{:S(2)}) async-start(bf16[3,128,1024]{1,0,2:T(4,128)(2,1)} %copy.77), calls=%async_computation.1 | async-start | bytes 2097152 | tf_op jit(solution)/shard_map/all_to_all | solution.py:174
  128.0 4.3 copy-start.15
  128.0 17.8 %all-to-all-start.2 = ((bf16[3,128,1024]{1,0,2:T(4,128)(2,1)}), bf16[3,128,1024]{1,0,2:T(4,128)(2,1)}, u32[]{:S(2)}, u32[]{:S(2)}) async-start(bf16[3,128,1024]{1,0,2:T(4,128)(2,1)} %copy.79), calls=%async_computation.2 | async-start | bytes 2097152 | tf_op jit(solution)/shard_map/all_to_all | solution.py:175
  145.8 24.9 %all-to-all-start = ((bf16[3,128,1024]{1,0,2:T(4,128)(2,1)}), bf16[3,128,1024]{1,0,2:T(4,128)(2,1)}, u32[]{:S(2)}, u32[]{:S(2)}) async-start(bf16[3,128,1024]{1,0,2:T(4,128)(2,1)} %copy.75), calls=%async_computation | async-start | bytes 2097152 | tf_op jit(solution)/shard_map/all_to_all | solution.py:176
  150.3 4.1 copy-start.16
  154.4 382.4 %collective-permute-start.2 = (bf16[4,512,1024]{2,1,0:T(8,128)(2,1)}, bf16[4,512,1024]{2,1,0:T(8,128)(2,1)}, u32[]{:S(2)}, u32[]{:S(2)}) collective-permute-start(bf16[4,512,1024]{2,1,0:T(8,128)(2,1)} %pad_maximum_fusion.1), channel_id=1, source_target_pairs={{0,16},{4,20},{8,24},{12,28},{16,0},{20,4},{24,8},{28,12},{1,17},{... | collective-permute-start | bytes 12582920 | tf_op jit(solution)/shard_map/ppermute | solution.py:20
  157.7 13.0 %copy-start.4 = (bf16[3,512,4,64]{1,3,2,0:T(8,128)(2,1)}, bf16[3,512,4,64]{1,3,2,0:T(8,128)(2,1)S(1)}, u32[]{:S(2)}) copy-start(bf16[3,512,4,64]{1,3,2,0:T(8,128)(2,1)S(1)} %reshape.215) | copy-start | bytes 2359300
  175.2 7.0 copy-start.17
  175.2 8.4 copy-start
  187.2 6.7 copy-start.37
  187.2 68.1 %copy-start.38 = (bf16[128]{0:T(256)(128)(2,1)S(1)}, bf16[128]{0:T(256)(128)(2,1)}, u32[]{:S(2)}) copy-start(bf16[128]{0:T(256)(128)(2,1)} %param.25) | copy-start | bytes 772
  187.2 294.8 %copy-start.39 = (bf16[128]{0:T(256)(128)(2,1)S(1)}, bf16[128]{0:T(256)(128)(2,1)}, u32[]{:S(2)}) copy-start(bf16[128]{0:T(256)(128)(2,1)} %param.26) | copy-start | bytes 772
  187.2 303.4 %copy-start.34 = (bf16[512]{0:T(512)(128)(2,1)S(1)}, bf16[512]{0:T(512)(128)(2,1)}, u32[]{:S(2)}) copy-start(bf16[512]{0:T(512)(128)(2,1)} %param.28) | copy-start | bytes 3076
  187.2 316.2 %copy-start.40 = (bf16[128]{0:T(256)(128)(2,1)S(1)}, bf16[128]{0:T(256)(128)(2,1)}, u32[]{:S(2)}) copy-start(bf16[128]{0:T(256)(128)(2,1)} %param.30) | copy-start | bytes 772
  187.3 325.3 %copy-start.41 = (bf16[128]{0:T(256)(128)(2,1)S(1)}, bf16[128]{0:T(256)(128)(2,1)}, u32[]{:S(2)}) copy-start(bf16[128]{0:T(256)(128)(2,1)} %param.31) | copy-start | bytes 772
  187.3 334.9 %copy-start.42 = (bf16[128]{0:T(256)(128)(2,1)S(1)}, bf16[128]{0:T(256)(128)(2,1)}, u32[]{:S(2)}) copy-start(bf16[128]{0:T(256)(128)(2,1)} %param.32) | copy-start | bytes 772
  189.7 341.6 %all-to-all-start.3 = ((bf16[3,512,256]{2,0,1:T(4,128)(2,1)}), bf16[3,512,256]{2,0,1:T(4,128)(2,1)S(1)}, u32[]{:S(2)}, u32[]{:S(2)}) async-start(bf16[3,512,256]{2,0,1:T(4,128)(2,1)} %copy.82), calls=%async_computation.3 | async-start | bytes 2097152 | tf_op jit(solution)/shard_map/all_to_all | solution.py:179
  532.1 3.2 copy-start.23
  532.2 4.6 copy-start.2
  542.5 7.6 copy-start.12
  550.1 21.7 %copy-start.6 = (bf16[8,512,1024]{2,1,0:T(8,128)(2,1)S(1)}, bf16[8,512,1024]{2,1,0:T(8,128)(2,1)}, u32[]{:S(2)}) copy-start(bf16[8,512,1024]{2,1,0:T(8,128)(2,1)} %pad_maximum_fusion) | copy-start | bytes 25165828
  571.8 3.6 copy-start.51
  576.5 7.4 copy-start.9
  585.0 15.2 %slice-start = ((s8[8388608]{0:T(1024)(128)(4,1)}), s8[4194304]{0:T(1024)(128)(4,1)S(1)}, s32[]{:S(2)}) async-start(s8[8388608]{0:T(1024)(128)(4,1)} %bitcast.221), calls=%async_computation.27 | async-start | bytes 8388608
  586.8 13.4 %copy-start.27 = (bf16[384,1024]{1,0:T(8,128)(2,1)}, bf16[384,1024]{1,0:T(8,128)(2,1)S(1)}, u32[]{:S(2)}) copy-start(bf16[384,1024]{1,0:T(8,128)(2,1)S(1)} %get-tuple-element.115) | copy-start | bytes 2359300
  586.8 13.4 %slice-start.1 = ((s8[8388608]{0:T(1024)(128)(4,1)}), s8[4194304]{0:T(1024)(128)(4,1)S(1)}, s32[]{:S(2)}) async-start(s8[8388608]{0:T(1024)(128)(4,1)} %bitcast.221), calls=%async_computation.28 | async-start | bytes 8388608
  600.2 4.0 copy-start.50
  604.2 1.7 copy-start.44
  608.4 18.1 %all-to-all-start.4 = ((bf16[3,128,1024]{1,0,2:T(4,128)(2,1)}), bf16[3,128,1024]{1,0,2:T(4,128)(2,1)S(1)}, u32[]{:S(2)}, u32[]{:S(2)}) async-start(bf16[3,128,1024]{1,0,2:T(4,128)(2,1)} %copy.85), calls=%async_computation.4 | async-start | bytes 2097152 | tf_op jit(solution)/shard_map/all_to_all | solution.py:321
  612.3 148.1 %reduce-scatter.23.cloned.1.call-start = ((), (), s32[]{:S(2)}) async-start(), calls=%async_computation.25 | async-start | bytes 2359296
  636.8 18.4 %copy-start.46 = (bf16[3,128,1024]{2,1,0:T(8,128)(2,1)S(1)}, bf16[3,128,1024]{2,1,0:T(8,128)(2,1)}, u32[]{:S(2)}) copy-start(bf16[3,128,1024]{2,1,0:T(8,128)(2,1)} %param.17) | copy-start | bytes 2359300
  661.8 100.5 %reduce-scatter.19.cloned.1.call-start = ((), (), s32[]{:S(2)}) async-start(), calls=%async_computation.23 | async-start | bytes 2359296
  668.5 6.9 copy-start.10
  675.4 3.0 copy-start.1
  680.7 17.4 %copy-start.47 = (bf16[3,128,1024]{2,1,0:T(8,128)(2,1)S(1)}, bf16[3,128,1024]{2,1,0:T(8,128)(2,1)}, u32[]{:S(2)}) copy-start(bf16[3,128,1024]{2,1,0:T(8,128)(2,1)} %param.17) | copy-start | bytes 2359300
  700.8 4.1 copy-start.5
  704.8 70.2 %reduce-scatter.21.cloned.1.call-start = ((), (), s32[]{:S(2)}) async-start(), calls=%async_computation.24 | async-start | bytes 2359296
  712.9 16.7 %copy-start.48 = (bf16[3,128,1024]{2,1,0:T(8,128)(2,1)S(1)}, bf16[3,128,1024]{2,1,0:T(8,128)(2,1)}, u32[]{:S(2)}) copy-start(bf16[3,128,1024]{2,1,0:T(8,128)(2,1)} %param.17) | copy-start | bytes 2359300
  732.2 4.1 copy-start.24
  736.3 75.9 %reduce-scatter.13.cloned.1.call-start = ((), (), s32[]{:S(2)}) async-start(), calls=%async_computation.20 | async-start | bytes 2359296 | tf_op jit(solution)/shard_map/reduce_scatter | solution.py:359
  740.1 162.6 %reduce-scatter.15.cloned.1.call-start = ((), (), s32[]{:S(2)}) async-start(), calls=%async_computation.21 | async-start | bytes 9437184 | tf_op jit(solution)/shard_map/reduce_scatter | solution.py:371
  750.5 242.4 %reduce-scatter.17.cloned.1.call-start = ((), (), s32[]{:S(2)}) async-start(), calls=%async_computation.22 | async-start | bytes 9437184 | tf_op jit(solution)/shard_map/reduce_scatter | solution.py:377
  760.4 233.8 %copy-start.49 = (u32[32]{0:T(128)S(1)}, u32[32]{0:T(128)}, u32[]{:S(2)}) copy-start(u32[32]{0:T(128)} %constant.109) | copy-start | bytes 388
  760.4 235.8 %copy-start.8 = (bf16[3,512,256]{2,1,0:T(8,128)(2,1)S(1)}, bf16[3,512,256]{2,1,0:T(8,128)(2,1)}, u32[]{:S(2)}) copy-start(bf16[3,512,256]{2,1,0:T(8,128)(2,1)} %copy-done.7) | copy-start | bytes 2359300
  760.4 323.4 %all-reduce.14.cloned.1.call-start = ((), (), s32[]{:S(2)}) async-start(), calls=%async_computation.26 | async-start | bytes 6291456 | tf_op jit(solution)/shard_map/psum | solution.py:391
  996.2 45.0 %copy-start.26 = (bf16[48,8,4,256]{3,1,2,0:T(8,128)(2,1)S(1)}, bf16[48,8,4,256]{3,1,2,0:T(8,128)(2,1)}, u32[]{:S(2)}) copy-start(bf16[48,8,4,256]{3,1,2,0:T(8,128)(2,1)} %copy-done.25) | copy-start | bytes 2359300
  1033.6 7.6 copy-start.43
  1041.2 1.8 copy-start.20
  1083.8 2.9 copy-start.21
  1083.8 4.5 copy-start.33
  1083.8 5.3 copy-start.32
  1086.7 3.4 copy-start.31
  1086.7 4.3 copy-start.30
  (11 other events, 11.6 us)
Sparse Core Ops, SparseCore 0:
  9.6 44.1 all-gather.17
  55.5 43.6 all-gather.19
  100.8 32.1 all-gather.15
  134.5 121.2 all-gather.21
  257.2 114.6 all-gather.23
  373.3 106.1 all-gather.25
  661.9 33.2 reduce-scatter.22
  704.9 33.4 reduce-scatter.18
  740.7 34.2 reduce-scatter.20
  777.7 34.4 reduce-scatter.12
  814.5 88.1 reduce-scatter.14
  904.9 87.9 reduce-scatter.16
  997.2 86.5 all-reduce.13
